TPU v7x, 256 devices: a whole 4x4x8 slice. The times are simulated.
256 devices in a mesh: period: 128 (over z, x, y), half: 2 (over core).
Axes of the slice: x: 4, y: 4, z: 8, core: 2. Of those that a mesh axis runs over, the one named last changes fastest.
Arguments:
- probes: float32 [1024, 4, 512], P('period', None, 'half'), may hold values from -6 to 6
- footprints: bfloat16 [1024, 512, 512], P('period', None, 'half'), may hold values from -0.25 to 0.25
- lag_weights: float32 [1024, 4], P('period'), may hold values from 0.2 to 2
- owners: int32 [1024, 4], P('period'), may hold values from 0 to 127, all different within a row; in each aligned block of 8 rows (0 to 7, 8 to 15, ...) at most 2 rows name the same one
- window_tiles: int32 [1024, 2], P('period', 'half'), may hold values from 0 to 10
- coords: int32 [2, 3072], replicated, may hold values from 0 to 63
- temporal: float32 [128, 128], replicated, as said below
Outputs:
- coefficients: float32 [4, 4], replicated
- residual: float32 [1024, 4, 512], P('period', None, 'half')
Inputs may be any that keep to these rules, and one draw needn't show every extreme that they name: `owners`: each row names 4 different periods. Among the 8 rows of one index of period, no period is named more than 2 times, and one is named exactly 2 times. `temporal`: symmetric.
All inputs are finite; a program needn't handle non-finite values.
Results may differ from a plain program's by a relative error of at most 0.025.
Values may be sent and summed in bfloat16 or wider, within the bound.
No kernel may reach another device: no remote copies, remote signals or barrier semaphores. Data moves between devices by JAX's collectives and lax.ppermute only.
A program may use at most 64 MiB of HBM per device.

v0:
```python
import jax
import jax.numpy as jnp
from jax import lax
from jax.sharding import PartitionSpec as P

epsilon = 1e-06
kernel_scale = 0.05
kernel_length = 6.0
highest = lax.Precision.HIGHEST


def from_partner(block, axis, bit):
    count = lax.axis_size(axis)
    route = []
    for low in range(count):
        high = low | 1 << bit
        if high != low and high < count:
            route += [(low, high), (high, low)]
    return lax.ppermute(block, axis, route)


def body(probes, footprints, lag_weights, owners, window_tiles, coords, temporal):
    periods = lax.axis_size("period")
    half_index = lax.axis_index("half")
    block_count, top_count = owners.shape
    probe_count = probes.shape[1]
    sound_count = footprints.shape[1]
    window = footprints.shape[2]
    win_tiles = window // 128
    cell_count = coords.shape[1]
    half_cells = cell_count // 2
    tile_count = half_cells // 128
    group_cells = half_cells // periods
    total_rows = float(block_count * periods * sound_count)
    tiles = window_tiles[:, 0]
    tile_hot = (
        tiles[:, None, None] + jnp.arange(win_tiles, dtype=jnp.int32)[None, :, None]
        == jnp.arange(tile_count, dtype=jnp.int32)[None, None, :]
    ).astype(jnp.float32)
    own_coords = lax.dynamic_slice_in_dim(coords, half_index * half_cells, half_cells, 1)
    delta_x = own_coords[0][:, None] - coords[0][None, :]
    delta_y = own_coords[1][:, None] - coords[1][None, :]
    squared = (delta_x * delta_x + delta_y * delta_y).astype(jnp.float32)
    kernel_rows = (kernel_scale * jnp.exp(-jnp.sqrt(squared) / kernel_length)).reshape(
        periods, group_cells, cell_count
    )
    owner_hot = (owners[:, :, None] == jnp.arange(periods, dtype=jnp.int32)[None, None, :]).astype(
        jnp.float32
    )

    def add_half(piece_rows):
        return jnp.einsum(
            "bps,bsw->bpw", piece_rows, footprints, preferred_element_type=jnp.float32
        )

    def mix_periods(grouped_part):
        mixed_part = jnp.einsum("ts,sik->tik", temporal, grouped_part, precision=highest)
        return lax.all_to_all(mixed_part, "period", split_axis=0, concat_axis=0, tiled=True)

    def apply_operator(vector):
        vector_low = vector.astype(jnp.bfloat16)
        partial_value = add_half(lax.all_gather(vector_low, "half", axis=2, tiled=True))
        terms = lag_weights[:, :, None, None] * partial_value[:, None, :, :]
        term_tiles = terms.reshape(block_count, top_count, probe_count, win_tiles, 128)
        placed = jnp.einsum("bjt,bkpjl->bkptl", tile_hot, term_tiles, precision=highest)
        dense_terms = jnp.einsum("bkn,bkptl->nptl", owner_hot, placed, precision=highest)
        summed = lax.psum_scatter(
            dense_terms.reshape(periods, probe_count, half_cells),
            "period",
            scatter_dimension=0,
            tiled=True,
        )
        flux_half = summed[0]
        other_half = from_partner(flux_half, "half", 0)
        whole_flux = jnp.where(
            half_index == 0,
            jnp.concatenate([flux_half, other_half], axis=1),
            jnp.concatenate([other_half, flux_half], axis=1),
        )
        grouped = jnp.einsum("pc,gkc->gpk", whole_flux, kernel_rows, precision=highest)
        mixed_flux = mix_periods(
            lax.all_to_all(grouped, "period", split_axis=0, concat_axis=0, tiled=True)
        )
        field_low = (
            jnp.transpose(mixed_flux, (1, 0, 2))
            .reshape(probe_count, half_cells)
            .astype(jnp.bfloat16)
        )
        field_all = lax.all_gather(field_low[None], "period", axis=0, tiled=True)
        selected = jnp.einsum(
            "bkn,npc->bkpc",
            owner_hot.astype(jnp.bfloat16),
            field_all,
            preferred_element_type=jnp.float32,
        )
        selected = selected.reshape(block_count, top_count, probe_count, tile_count, 128)
        windows = jnp.einsum("bkptl,bjt->bkpjl", selected, tile_hot, precision=highest)
        windows = windows.astype(jnp.bfloat16).reshape(block_count, top_count, probe_count, window)
        products = jnp.einsum(
            "bkpw,bsw->bkps", windows, footprints, preferred_element_type=jnp.float32
        )
        sounded = jnp.einsum("bk,bkps->bps", lag_weights, products, precision=highest)
        return lax.psum_scatter(
            sounded.astype(jnp.bfloat16), "half", scatter_dimension=2, tiled=True
        ).astype(jnp.float32)

    def local_mean(values):
        return jnp.sum(values, axis=(0, 2))

    def lanczos_step(current, image):
        inner_sum = lax.psum(local_mean(current * image), ("period", "half"))
        alpha = inner_sum / total_rows
        remainder = image - alpha[None, :, None] * current
        square_sum = lax.psum(local_mean(remainder * remainder), ("period", "half"))
        beta = jnp.sqrt(square_sum / total_rows + epsilon)
        return (alpha, remainder, beta)

    start_sum = lax.psum(local_mean(probes * probes), ("period", "half"))
    first_q = probes / jnp.sqrt(start_sum / total_rows + epsilon)[None, :, None]
    image_one = apply_operator(first_q)
    alpha_one, rest_one, beta_one = lanczos_step(first_q, image_one)
    second_q = rest_one / beta_one[None, :, None]
    image_two = apply_operator(second_q) - beta_one[None, :, None] * first_q
    alpha_two, residual, beta_two = lanczos_step(second_q, image_two)
    coefficients = jnp.stack([alpha_one, beta_one, alpha_two, beta_two], axis=0)
    return (coefficients, residual)


def solution(mesh):
    in_specs = (
        P("period", None, "half"),
        P("period", None, "half"),
        P("period", None),
        P("period", None),
        P("period", "half"),
        P(),
        P(),
    )
    out_specs = (P(), P("period", None, "half"))
    return jax.shard_map(body, mesh=mesh, in_specs=in_specs, out_specs=out_specs, check_vma=False)
```

profile of v0, /device:TPU:1, one launch (start us, length us, event | category | flops | bytes accessed | tf_op | source)
XLA Modules:
  0.0 1305.8 jit_solution(13119377155676004425)
XLA Ops:
  7.2 1.0 multiply_reduce_fusion.3
  8.3 81.4 %psum.35 = f32[4]{0:T(128)S(1)} all-reduce(f32[4]{0:T(128)S(1)} %multiply_reduce_fusion.3), channel_id=1, replica_groups=mesh['period'=128,'half'=2] {'period','half'}, use_global_device_ids=true, to_apply=%region_1.0 | all-reduce | flops 4 | bytes 32 | tf_op jit(solution)/shard_map/psum | solution.py:118
  89.7 0.7 iota_add_fusion
  90.4 0.8 copy.24
  91.2 0.8 fusion.101
  92.0 2.5 all_gather.12
  94.5 0.4 fusion.103
  94.9 0.8 convolution_bitcast_fusion.1
  95.7 4.4 fusion.38
  100.1 5.1 copy.26
  105.3 0.6 copy-done.5
  105.9 0.6 dynamic-slice
  106.4 221.5 %all-reduce.5.cloned.1.call-done = f32[128,4,1536]{2,1,0:T(4,128)} async-done(((f32[128,4,1536]{2,1,0:T(4,128)}), f32[128,4,1536]{2,1,0:T(4,128)}) %all-reduce.5.cloned.1.call-update) | async-done | bytes 3145744
  328.0 1.4 dynamic-slice_bitcast_fusion.1
  329.4 4.9 collective-permute-start
  334.8 0.4 collective-permute-done
  335.2 46.6 %fusion.32 = f32[128,4,12]{0,1,2:T(4,128)S(1)} fusion(s32[3072]{0:T(1024)S(1)} %bitcast.132, s32[128,12]{0,1:T(8,128)S(1)} %copy.23, s32[3072]{0:T(1024)S(1)} %bitcast.130, s32[128,12]{0,1:T(8,128)S(1)} %copy.22, f32[4,1536]{1,0:T(4,128)S(1)} %collective-permute-done, f32[4,1536]{1,0:T(4,128)S(1)} %dynamic-slice_bitcast_fusion.1, pred[]{:T(512)S(6)} %eq.36), kind=kOutput, calls=%fused_computation.35 | convolution fusion | flops 268996608 | bytes 110593 | tf_op jit(solution)/shard_map/pc,gkc->gpk/dot_general | solution.py:80
  382.0 23.7 %all_to_all.20 = f32[128,4,12]{2,1,0:T(4,128)S(1)} all-to-all(f32[128,4,12]{2,1,0:T(4,128)S(1)} %copy.27), channel_id=1, replica_groups=mesh['period'=128,'half'=2] {'period'}, dimensions={0} | all-to-all | bytes 49152 | tf_op jit(solution)/shard_map/all_to_all | solution.py:82
  405.7 0.5 convolution_bitcast_fusion.3
  406.4 17.2 %all_to_all.21 = bf16[128,4,12]{2,1,0:T(4,128)(2,1)S(1)} all-to-all(bf16[128,4,12]{2,1,0:T(4,128)(2,1)S(1)} %copy.29), channel_id=1, replica_groups=mesh['period'=128,'half'=2] {'period'}, dimensions={0} | all-to-all | bytes 24576 | tf_op jit(solution)/shard_map/all_to_all | solution.py:58
  423.7 0.8 convert_element_type.80
  424.5 0.2 reduce-scatter.7.cloned.1.call-start
  424.8 94.2 %all-gather.3.cloned.1.call-done = bf16[128,4,1536]{2,1,0:T(4,128)(2,1)} async-done(((bf16[1,4,1536]{2,1,0:T(4,128)(2,1)}), bf16[128,4,1536]{2,1,0:T(4,128)(2,1)}) %all-gather.3.cloned.1.call-update) | async-done | bytes 1572880 | tf_op jit(solution)/shard_map/all_gather | solution.py:89
  519.0 2.0 fusion.24
  521.1 0.5 fusion.30
  521.7 0.6 fusion.16
  522.3 0.6 fusion.42
  523.0 0.7 copy.52
  523.7 1.3 reshape.130
  525.1 16.9 %reduce-scatter.7.cloned.1.call-done = bf16[256,32]{1,0:T(8,128)(2,1)} async-done(((bf16[512,32]{1,0:T(8,128)(2,1)}), bf16[256,32]{1,0:T(8,128)(2,1)}) %reduce-scatter.7.cloned.1.call-update) | async-done | bytes 16400
  542.0 1.2 reshape.131
  543.2 0.4 copy.53
  543.7 77.4 %psum.36 = f32[4]{0:T(128)S(1)} all-reduce(f32[4]{0:T(128)S(1)} %fusion.68), channel_id=1, replica_groups=mesh['period'=128,'half'=2] {'period','half'}, use_global_device_ids=true, to_apply=%region_5.6 | all-reduce | flops 4 | bytes 32 | tf_op jit(solution)/shard_map/psum | solution.py:111
  621.1 0.2 multiply_reduce_fusion.2
  621.3 73.1 %psum.37 = f32[4]{0:T(128)S(1)} all-reduce(f32[4]{0:T(128)S(1)} %multiply_reduce_fusion.2), channel_id=1, replica_groups=mesh['period'=128,'half'=2] {'period','half'}, use_global_device_ids=true, to_apply=%region_7.8 | all-reduce | flops 4 | bytes 32 | tf_op jit(solution)/shard_map/psum | solution.py:114
  694.5 2.2 all_gather.14
  696.7 0.4 fusion.104
  697.1 0.8 convolution_bitcast_fusion
  697.9 4.4 fusion.36
  702.3 5.1 copy.34
  707.5 223.8 %all-reduce.7.cloned.1.call-done = f32[128,4,1536]{2,1,0:T(4,128)} async-done(((f32[128,4,1536]{2,1,0:T(4,128)}), f32[128,4,1536]{2,1,0:T(4,128)}) %all-reduce.7.cloned.1.call-update) | async-done | bytes 3145744
  931.3 1.4 dynamic-slice_bitcast_fusion
  932.7 4.9 collective-permute-start.1
  937.6 0.8 collective-permute-done.1
  938.5 46.6 %fusion.33 = f32[128,4,12]{0,1,2:T(4,128)S(1)} fusion(s32[3072]{0:T(1024)S(1)} %bitcast.133, s32[128,12]{0,1:T(8,128)S(1)} %copy.23, s32[3072]{0:T(1024)S(1)} %bitcast.131, s32[128,12]{0,1:T(8,128)S(1)} %copy.22, f32[4,1536]{1,0:T(4,128)S(1)} %collective-permute-done.1, f32[4,1536]{1,0:T(4,128)S(1)} %dynamic-slice_bitcast_fusion, pred[]{:T(512)S(6)} %eq.36), kind=kOutput, calls=%fused_computation.36 | convolution fusion | flops 268996608 | bytes 110593 | tf_op jit(solution)/shard_map/pc,gkc->gpk/dot_general | solution.py:80
  985.3 23.7 %all_to_all.22 = f32[128,4,12]{2,1,0:T(4,128)S(1)} all-to-all(f32[128,4,12]{2,1,0:T(4,128)S(1)} %copy.35), channel_id=1, replica_groups=mesh['period'=128,'half'=2] {'period'}, dimensions={0} | all-to-all | bytes 49152 | tf_op jit(solution)/shard_map/all_to_all | solution.py:82
  1009.0 0.5 convolution_bitcast_fusion.2
  1009.7 17.2 %all_to_all.23 = bf16[128,4,12]{2,1,0:T(4,128)(2,1)S(1)} all-to-all(bf16[128,4,12]{2,1,0:T(4,128)(2,1)S(1)} %copy.37), channel_id=1, replica_groups=mesh['period'=128,'half'=2] {'period'}, dimensions={0} | all-to-all | bytes 24576 | tf_op jit(solution)/shard_map/all_to_all | solution.py:58
  1027.0 0.8 convert_element_type.88
  1027.9 94.5 %all-gather.5.cloned.1.call-done = bf16[128,4,1536]{2,1,0:T(4,128)(2,1)} async-done(((bf16[1,4,1536]{2,1,0:T(4,128)(2,1)}), bf16[128,4,1536]{2,1,0:T(4,128)(2,1)}) %all-gather.5.cloned.1.call-update) | async-done | bytes 1572880 | tf_op jit(solution)/shard_map/all_gather | solution.py:89
  1122.3 2.0 fusion.27
  1124.4 0.5 fusion.31
  1125.0 0.6 fusion.14
  1125.6 0.6 fusion.40
  1126.3 0.7 copy.54
  1127.0 1.3 reshape.132
  1128.4 16.9 %reduce-scatter.9.cloned.1.call-done = bf16[256,32]{1,0:T(8,128)(2,1)} async-done(((bf16[512,32]{1,0:T(8,128)(2,1)}), bf16[256,32]{1,0:T(8,128)(2,1)}) %reduce-scatter.9.cloned.1.call-update) | async-done | bytes 16400
  1145.3 1.2 reshape.133
  1146.5 0.4 copy.55
  1146.8 0.2 multiply_reduce_fusion.1
  1147.0 77.4 %psum.38 = f32[4]{0:T(128)S(1)} all-reduce(f32[4]{0:T(128)S(1)} %multiply_reduce_fusion.1), channel_id=1, replica_groups=mesh['period'=128,'half'=2] {'period','half'}, use_global_device_ids=true, to_apply=%region_11.12 | all-reduce | flops 4 | bytes 32 | tf_op jit(solution)/shard_map/psum | solution.py:111
  1224.5 0.8 multiply_reduce_fusion
  1225.3 73.1 %psum.39 = f32[4]{0:T(128)S(1)} all-reduce(f32[4]{0:T(128)S(1)} %get-tuple-element.4), channel_id=1, replica_groups=mesh['period'=128,'half'=2] {'period','half'}, use_global_device_ids=true, to_apply=%region_13.14 | all-reduce | flops 4 | bytes 32 | tf_op jit(solution)/shard_map/psum | solution.py:114
  1298.4 0.6 pad_maximum_fusion
  (48 shorter events, 2.1 us)
Async XLA Ops:
  7.2 87.3 %copy-start = (bf16[8,512,256]{2,1,0:T(8,128)(2,1)S(1)}, bf16[8,512,256]{2,1,0:T(8,128)(2,1)}, u32[]{:S(2)}) copy-start(bf16[8,512,256]{2,1,0:T(8,128)(2,1)} %param.8) | copy-start | bytes 6291460
  7.2 88.5 %copy-start.3 = (s32[8,4]{0,1:T(4,128)S(1)}, s32[8,4]{0,1:T(4,128)}, u32[]{:S(2)}) copy-start(s32[8,4]{0,1:T(4,128)} %param.10) | copy-start | bytes 388
  7.2 320.8 %all-reduce.5.cloned.1.call-start = ((), (), s32[]{:S(2)}) async-start(), calls=%async_computation.10 | async-start | bytes 6291456
  105.2 0.7 copy-start.5
  105.2 229.1 %copy-start.2 = (s32[2,3072]{1,0:T(2,128)S(1)}, s32[2,3072]{1,0:T(2,128)}, u32[]{:S(2)}) copy-start(s32[2,3072]{1,0:T(2,128)} %param.12) | copy-start | bytes 73732
  105.2 413.8 %all-gather.3.cloned.1.call-start = ((), (), s32[]{:S(2)}) async-start(), calls=%async_computation.6 | async-start | bytes 1585152 | tf_op jit(solution)/shard_map/all_gather | solution.py:89
  329.4 5.8 collective-permute-start
  335.2 70.5 %copy-start.1 = (f32[128,128]{1,0:T(8,128)S(1)}, f32[128,128]{1,0:T(8,128)}, u32[]{:S(2)}) copy-start(f32[128,128]{1,0:T(8,128)} %param.13) | copy-start | bytes 196612
  335.2 89.6 %copy-start.4 = (f32[8,4]{0,1:T(4,128)S(1)}, f32[8,4]{0,1:T(4,128)}, u32[]{:S(2)}) copy-start(f32[8,4]{0,1:T(4,128)} %param.9) | copy-start | bytes 388
  424.5 117.5 %reduce-scatter.7.cloned.1.call-start = ((), (), s32[]{:S(2)}) async-start(), calls=%async_computation.8 | async-start | bytes 196608
  525.0 406.2 %all-reduce.7.cloned.1.call-start = ((), (), s32[]{:S(2)}) async-start(), calls=%async_computation.11 | async-start | bytes 6291456
  707.4 414.9 %all-gather.5.cloned.1.call-start = ((), (), s32[]{:S(2)}) async-start(), calls=%async_computation.7 | async-start | bytes 1585152 | tf_op jit(solution)/shard_map/all_gather | solution.py:89
  932.7 5.8 collective-permute-start.1
  1027.8 117.5 %reduce-scatter.9.cloned.1.call-start = ((), (), s32[]{:S(2)}) async-start(), calls=%async_computation.9 | async-start | bytes 196608
Sparse Core Ops, SparseCore 0:
  105.3 222.5 all-reduce.4
  424.6 94.3 all-gather.2
  525.2 16.7 reduce-scatter.6
  707.5 223.6 all-reduce.6
  1027.9 94.3 all-gather.4
  1128.5 16.7 reduce-scatter.8
where the time goes:
time: 1310 us
  waiting for transfers between devices  669 us (51%)
  blocking collectives  469 us (36%)
  matrix products  113 us (9%)
  local copies, waits for them, and re-layouts  25.2 us (2%)
  between operations  14.4 us (1%)
    unnamed x10, waiting for transfers between devices  479 us
    all_gather x2, waiting for transfers between devices, apply_operator(): field_all = lax.all_gather(field_low[None], 'period', axis=0, tiled=True)  189 us
    psum x2, blocking collectives, lanczos_step(): inner_sum = lax.psum(local_mean(current * image), ('period', 'half'))  155 us
    psum x2, blocking collectives, lanczos_step(): square_sum = lax.psum(local_mean(remainder * remainder), ('period', 'half'))  146 us
    dot_general x2, matrix products, apply_operator(): jnp.einsum('pc,gkc->gpk', whole_flux, kernel_rows, precision=highest)  93.3 us
    psum x1, blocking collectives, body(): start_sum = lax.psum(local_mean(probes * probes), ('period', 'half'))  81.4 us
    all_to_all x2, blocking collectives, apply_operator(): lax.all_to_all(grouped, 'period', split_axis=0, concat_axis=0, tiled=True)  47.4 us
    all_to_all x2, blocking collectives, mix_periods(): lax.all_to_all(mixed_part, 'period', split_axis=0, concat_axis=0, tiled=T...  34.5 us
  transfers between devices with their start and end apart: 8, of which 8 were waited for; matrix products, arithmetic and copies ran while one was open for 0% of the time, Pallas kernels for 0%

commit v1 on v0

--- a/solution.py
+++ b/solution.py
@@ -7,6 +7,11 @@
 kernel_scale = 0.05
 kernel_length = 6.0
 highest = lax.Precision.HIGHEST
+
+
+def one_after_other(value, first, second):
+    inner = lax.psum(value, first)
+    return lax.psum(inner, second)
 
 
 def from_partner(block, axis, bit):
@@ -111,7 +116,7 @@
         inner_sum = lax.psum(local_mean(current * image), ("period", "half"))
         alpha = inner_sum / total_rows
         remainder = image - alpha[None, :, None] * current
-        square_sum = lax.psum(local_mean(remainder * remainder), ("period", "half"))
+        square_sum = one_after_other(local_mean(remainder * remainder), "period", "half")
         beta = jnp.sqrt(square_sum / total_rows + epsilon)
         return (alpha, remainder, beta)
 

time: 1310 us -> 1850 us (1.41)
  blocking collectives: 469 us -> 1020 us
    psum x2 -> x4, blocking collectives: 146 us -> 696 us  [the longest x2 579 us: one_after_other(): inner = lax.psum(value, first)]
where the time goes in v1:
time: 1850 us
  blocking collectives  1020 us (55%)
  waiting for transfers between devices  667 us (36%)
  matrix products  113 us (6%)
  local copies, waits for them, and re-layouts  25.2 us (1%)
    psum x2, blocking collectives, one_after_other(): inner = lax.psum(value, first)  579 us
    unnamed x10, waiting for transfers between devices  477 us
    all_gather x2, waiting for transfers between devices, apply_operator(): field_all = lax.all_gather(field_low[None], 'period', axis=0, tiled=True)  189 us
    psum x2, blocking collectives, lanczos_step(): inner_sum = lax.psum(local_mean(current * image), ('period', 'half'))  155 us
    psum x2, blocking collectives, one_after_other(): return lax.psum(inner, second)  116 us
    dot_general x2, matrix products, apply_operator(): jnp.einsum('pc,gkc->gpk', whole_flux, kernel_rows, precision=highest)  93.3 us
    psum x1, blocking collectives, body(): start_sum = lax.psum(local_mean(probes * probes), ('period', 'half'))  81.4 us
    all_to_all x2, blocking collectives, apply_operator(): lax.all_to_all(grouped, 'period', split_axis=0, concat_axis=0, tiled=True)  47.4 us
  transfers between devices with their start and end apart: 8, of which 8 were waited for; matrix products, arithmetic and copies ran while one was open for 0% of the time, Pallas kernels for 0%

profile of v1, /device:TPU:1, one launch (start us, length us, event | category | flops | bytes accessed | tf_op | source)
XLA Modules:
  0.0 1853.3 jit_solution(3794682644688899739)
XLA Ops:
  7.2 1.0 multiply_reduce_fusion.3
  8.3 81.4 %psum.49 = f32[4]{0:T(128)S(1)} all-reduce(f32[4]{0:T(128)S(1)} %multiply_reduce_fusion.3), channel_id=1, replica_groups=mesh['period'=128,'half'=2] {'period','half'}, use_global_device_ids=true, to_apply=%region_1.0 | all-reduce | flops 4 | bytes 32 | tf_op jit(solution)/shard_map/psum | solution.py:123
  89.7 0.7 iota_add_fusion
  90.4 0.8 copy.24
  91.2 0.8 fusion.101
  92.0 2.5 all_gather.12
  94.5 0.4 fusion.103
  94.9 0.8 convolution_bitcast_fusion.1
  95.7 4.4 fusion.38
  100.1 5.1 copy.26
  105.3 0.6 copy-done.5
  105.9 0.6 dynamic-slice
  106.4 221.5 %all-reduce.5.cloned.1.call-done = f32[128,4,1536]{2,1,0:T(4,128)} async-done(((f32[128,4,1536]{2,1,0:T(4,128)}), f32[128,4,1536]{2,1,0:T(4,128)}) %all-reduce.5.cloned.1.call-update) | async-done | bytes 3145744
  328.0 1.4 dynamic-slice_bitcast_fusion.1
  329.4 4.9 collective-permute-start
  334.8 0.4 collective-permute-done
  335.2 46.6 %fusion.32 = f32[128,4,12]{0,1,2:T(4,128)S(1)} fusion(s32[3072]{0:T(1024)S(1)} %bitcast.132, s32[128,12]{0,1:T(8,128)S(1)} %copy.23, s32[3072]{0:T(1024)S(1)} %bitcast.130, s32[128,12]{0,1:T(8,128)S(1)} %copy.22, f32[4,1536]{1,0:T(4,128)S(1)} %collective-permute-done, f32[4,1536]{1,0:T(4,128)S(1)} %dynamic-slice_bitcast_fusion.1, pred[]{:T(512)S(6)} %eq.36), kind=kOutput, calls=%fused_computation.35 | convolution fusion | flops 268996608 | bytes 110593 | tf_op jit(solution)/shard_map/pc,gkc->gpk/dot_general | solution.py:85
  382.0 23.7 %all_to_all.20 = f32[128,4,12]{2,1,0:T(4,128)S(1)} all-to-all(f32[128,4,12]{2,1,0:T(4,128)S(1)} %copy.27), channel_id=1, replica_groups=mesh['period'=128,'half'=2] {'period'}, dimensions={0} | all-to-all | bytes 49152 | tf_op jit(solution)/shard_map/all_to_all | solution.py:87
  405.7 0.5 convolution_bitcast_fusion.3
  406.4 17.2 all_to_all.21
  423.7 0.8 convert_element_type.80
  424.5 0.2 reduce-scatter.7.cloned.1.call-start
  424.8 94.2 %all-gather.3.cloned.1.call-done = bf16[128,4,1536]{2,1,0:T(4,128)(2,1)} async-done(((bf16[1,4,1536]{2,1,0:T(4,128)(2,1)}), bf16[128,4,1536]{2,1,0:T(4,128)(2,1)}) %all-gather.3.cloned.1.call-update) | async-done | bytes 1572880 | tf_op jit(solution)/shard_map/all_gather | solution.py:94
  519.0 2.0 fusion.24
  521.1 0.5 fusion.30
  521.7 0.6 fusion.16
  522.3 0.6 fusion.42
  523.0 0.7 copy.52
  523.7 1.3 reshape.130
  525.1 16.9 reduce-scatter.7.cloned.1.call-done
  542.0 1.2 reshape.131
  543.2 0.4 copy.53
  543.7 77.4 %psum.50 = f32[4]{0:T(128)S(1)} all-reduce(f32[4]{0:T(128)S(1)} %fusion.68), channel_id=1, replica_groups=mesh['period'=128,'half'=2] {'period','half'}, use_global_device_ids=true, to_apply=%region_5.6 | all-reduce | flops 4 | bytes 32 | tf_op jit(solution)/shard_map/psum | solution.py:116
  621.3 289.7 %psum.51 = f32[4]{0:T(128)S(1)} all-reduce(f32[4]{0:T(128)S(1)} %multiply_reduce_fusion.2), channel_id=1, replica_groups=mesh['period'=128,'half'=2] {'period'}, use_global_device_ids=true, to_apply=%region_7.8 | all-reduce | flops 4 | bytes 32 | tf_op jit(solution)/shard_map/psum | solution.py:13
  911.0 58.2 %psum.52 = f32[4]{0:T(128)S(1)} all-reduce(f32[4]{0:T(128)S(1)} %psum.51), channel_id=1, replica_groups=mesh['period'=128,'half'=2] {'half'}, use_global_device_ids=true, to_apply=%region_8.9 | all-reduce | flops 4 | bytes 32 | tf_op jit(solution)/shard_map/psum | solution.py:14
  969.3 1.9 all_gather.14
  971.1 0.4 fusion.104
  971.6 0.8 convolution_bitcast_fusion
  972.4 4.4 fusion.36
  976.7 5.1 copy.34
  981.9 222.0 %all-reduce.7.cloned.1.call-done = f32[128,4,1536]{2,1,0:T(4,128)} async-done(((f32[128,4,1536]{2,1,0:T(4,128)}), f32[128,4,1536]{2,1,0:T(4,128)}) %all-reduce.7.cloned.1.call-update) | async-done | bytes 3145744
  1204.0 1.4 dynamic-slice_bitcast_fusion
  1205.3 4.9 collective-permute-start.1
  1210.3 0.8 collective-permute-done.1
  1211.1 46.6 %fusion.33 = f32[128,4,12]{0,1,2:T(4,128)S(1)} fusion(s32[3072]{0:T(1024)S(1)} %bitcast.133, s32[128,12]{0,1:T(8,128)S(1)} %copy.23, s32[3072]{0:T(1024)S(1)} %bitcast.131, s32[128,12]{0,1:T(8,128)S(1)} %copy.22, f32[4,1536]{1,0:T(4,128)S(1)} %collective-permute-done.1, f32[4,1536]{1,0:T(4,128)S(1)} %dynamic-slice_bitcast_fusion, pred[]{:T(512)S(6)} %eq.36), kind=kOutput, calls=%fused_computation.36 | convolution fusion | flops 268996608 | bytes 110593 | tf_op jit(solution)/shard_map/pc,gkc->gpk/dot_general | solution.py:85
  1258.0 23.7 %all_to_all.22 = f32[128,4,12]{2,1,0:T(4,128)S(1)} all-to-all(f32[128,4,12]{2,1,0:T(4,128)S(1)} %copy.35), channel_id=1, replica_groups=mesh['period'=128,'half'=2] {'period'}, dimensions={0} | all-to-all | bytes 49152 | tf_op jit(solution)/shard_map/all_to_all | solution.py:87
  1281.7 0.5 convolution_bitcast_fusion.2
  1282.4 17.2 all_to_all.23
  1299.7 0.8 convert_element_type.88
  1300.5 94.5 %all-gather.5.cloned.1.call-done = bf16[128,4,1536]{2,1,0:T(4,128)(2,1)} async-done(((bf16[1,4,1536]{2,1,0:T(4,128)(2,1)}), bf16[128,4,1536]{2,1,0:T(4,128)(2,1)}) %all-gather.5.cloned.1.call-update) | async-done | bytes 1572880 | tf_op jit(solution)/shard_map/all_gather | solution.py:94
  1395.0 2.0 fusion.27
  1397.0 0.5 fusion.31
  1397.7 0.6 fusion.14
  1398.3 0.6 fusion.40
  1399.0 0.7 copy.54
  1399.7 1.3 reshape.132
  1401.0 16.9 reduce-scatter.9.cloned.1.call-done
  1418.0 1.2 reshape.133
  1419.2 0.4 copy.55
  1419.7 77.4 %psum.53 = f32[4]{0:T(128)S(1)} all-reduce(f32[4]{0:T(128)S(1)} %multiply_reduce_fusion.1), channel_id=1, replica_groups=mesh['period'=128,'half'=2] {'period','half'}, use_global_device_ids=true, to_apply=%region_12.13 | all-reduce | flops 4 | bytes 32 | tf_op jit(solution)/shard_map/psum | solution.py:116
  1497.1 0.8 multiply_reduce_fusion
  1497.9 289.7 %psum.54 = f32[4]{0:T(128)S(1)} all-reduce(f32[4]{0:T(128)S(1)} %get-tuple-element.4), channel_id=1, replica_groups=mesh['period'=128,'half'=2] {'period'}, use_global_device_ids=true, to_apply=%region_14.15 | all-reduce | flops 4 | bytes 32 | tf_op jit(solution)/shard_map/psum | solution.py:13
  1787.6 58.2 %psum.55 = f32[4]{0:T(128)S(1)} all-reduce(f32[4]{0:T(128)S(1)} %psum.54), channel_id=1, replica_groups=mesh['period'=128,'half'=2] {'half'}, use_global_device_ids=true, to_apply=%region_15.16 | all-reduce | flops 4 | bytes 32 | tf_op jit(solution)/shard_map/psum | solution.py:14
  1845.8 0.6 pad_maximum_fusion
  (50 shorter events, 2.5 us)
Async XLA Ops:
  7.2 87.3 %copy-start = (bf16[8,512,256]{2,1,0:T(8,128)(2,1)S(1)}, bf16[8,512,256]{2,1,0:T(8,128)(2,1)}, u32[]{:S(2)}) copy-start(bf16[8,512,256]{2,1,0:T(8,128)(2,1)} %param.8) | copy-start | bytes 6291460
  7.2 88.5 %copy-start.3 = (s32[8,4]{0,1:T(4,128)S(1)}, s32[8,4]{0,1:T(4,128)}, u32[]{:S(2)}) copy-start(s32[8,4]{0,1:T(4,128)} %param.10) | copy-start | bytes 388
  7.2 320.8 %all-reduce.5.cloned.1.call-start = ((), (), s32[]{:S(2)}) async-start(), calls=%async_computation.10 | async-start | bytes 6291456
  105.2 0.7 copy-start.5
  105.2 229.1 %copy-start.2 = (s32[2,3072]{1,0:T(2,128)S(1)}, s32[2,3072]{1,0:T(2,128)}, u32[]{:S(2)}) copy-start(s32[2,3072]{1,0:T(2,128)} %param.12) | copy-start | bytes 73732
  105.2 413.8 %all-gather.3.cloned.1.call-start = ((), (), s32[]{:S(2)}) async-start(), calls=%async_computation.6 | async-start | bytes 1585152 | tf_op jit(solution)/shard_map/all_gather | solution.py:94
  329.4 5.8 collective-permute-start
  335.2 70.5 %copy-start.1 = (f32[128,128]{1,0:T(8,128)S(1)}, f32[128,128]{1,0:T(8,128)}, u32[]{:S(2)}) copy-start(f32[128,128]{1,0:T(8,128)} %param.13) | copy-start | bytes 196612
  335.2 89.6 %copy-start.4 = (f32[8,4]{0,1:T(4,128)S(1)}, f32[8,4]{0,1:T(4,128)}, u32[]{:S(2)}) copy-start(f32[8,4]{0,1:T(4,128)} %param.9) | copy-start | bytes 388
  424.5 117.5 %reduce-scatter.7.cloned.1.call-start = ((), (), s32[]{:S(2)}) async-start(), calls=%async_computation.8 | async-start | bytes 196608
  525.0 678.9 %all-reduce.7.cloned.1.call-start = ((), (), s32[]{:S(2)}) async-start(), calls=%async_computation.11 | async-start | bytes 6291456
  981.9 413.1 %all-gather.5.cloned.1.call-start = ((), (), s32[]{:S(2)}) async-start(), calls=%async_computation.7 | async-start | bytes 1585152 | tf_op jit(solution)/shard_map/all_gather | solution.py:94
  1205.3 5.8 collective-permute-start.1
  1300.5 117.5 %reduce-scatter.9.cloned.1.call-start = ((), (), s32[]{:S(2)}) async-start(), calls=%async_computation.9 | async-start | bytes 196608
Sparse Core Ops, SparseCore 0:
  105.3 222.5 all-reduce.4
  424.6 94.3 all-gather.2
  525.2 16.7 reduce-scatter.6
  982.0 221.9 all-reduce.6
  1300.6 94.3 all-gather.4
  1401.2 16.7 reduce-scatter.8
